TPU v7x, 32 devices: a whole 2x2x4 slice. The times are simulated.
32 devices in a mesh: grp: 2 (over y), seq: 4 (over z), req: 2 (over x), hd: 2 (over core).
Axes of the slice: x: 2, y: 2, z: 4, core: 2. Of those that a mesh axis runs over, the one named last changes fastest.
Arguments:
- cache: bfloat16 [8, 8, 1536, 256], P(('grp', 'req'), 'hd', 'seq'), parts along dimension 0, may hold values from -7 to 7
- evicted: bfloat16 [8, 8, 256, 256], P(('grp', 'req'), 'hd', 'seq'), parts along dimension 0, may hold values from -6 to 6
- merge_weight: bfloat16 [8, 8, 256], P(('grp', 'req'), 'hd', 'seq'), parts along dimension 0, may hold values from 0.25 to 2.5
- targets: int32 [8, 8, 256], P(('grp', 'req'), 'hd', 'seq'), parts along dimension 0, may hold values from 0 to 1535, as said below
- kept_counts: int32 [8, 4], P(('grp', 'req'), 'seq'), parts along dimension 0, may hold values from 192 to 384, as said below
- queries: bfloat16 [4, 8, 64, 128], P(None, ('grp', 'req'), 'hd'), parts along dimension 1, may hold values from -1024 to 1024
- new_rows: bfloat16 [4, 8, 8, 256], P(None, ('grp', 'req'), 'hd'), parts along dimension 1, may hold values from -8 to 8
Outputs:
- merged_cache: bfloat16 [8, 8, 1536, 256], P(('grp', 'req'), 'hd', 'seq'), parts along dimension 0
- attended: bfloat16 [4, 8, 64, 128], P(None, ('grp', 'req'), 'hd'), parts along dimension 1
There are 2 independent parts, one for each index of `grp`. A program takes and returns all parts, laid end to end along the dimension named above; each array names one. Nothing has to cross between parts.
Inputs may be any that keep to these rules, and one draw needn't show every extreme that they name: `targets`: for each request, head and block of 64 evicted rows, at most 32 rows target one block of 384 kept positions; every target is a live position. `kept_counts`: each request has a block with all 384 positions live.
All inputs are finite; a program needn't handle non-finite values.
Results may differ from a plain program's by a relative error of at most 0.0029.
Values may be sent and summed in bfloat16 or wider, within the bound.
A program may use at most 64 MiB of HBM per device.

v0:
```python
import math

import jax
import jax.numpy as jnp
from jax import lax
from jax.sharding import PartitionSpec as P


def combined_all(part, axis, combine):
    gathered = jax.tree.map(lambda a: lax.all_gather(a, axis), part)

    def take(source):
        return jax.tree.map(lambda a: lax.dynamic_index_in_dim(a, source, 0, False), gathered)

    return lax.fori_loop(
        1, lax.axis_size(axis), lambda source, state: combine(state, take(source)), take(0)
    )


def combine_parts(former, latter):
    former_max, former_sum, former_acc = former
    latter_max, latter_sum, latter_acc = latter
    highest = jnp.maximum(former_max, latter_max)
    former_scale = jnp.exp(former_max - highest)
    latter_scale = jnp.exp(latter_max - highest)
    return (
        highest,
        former_sum * former_scale + latter_sum * latter_scale,
        former_acc * former_scale[..., None] + latter_acc * latter_scale[..., None],
    )


def spread_rows(received, weights, positions, kept_dev):
    columns = jnp.arange(kept_dev, dtype=jnp.int32)
    placing = jnp.where(
        positions[..., None] == columns, weights[..., None], jnp.zeros((), jnp.bfloat16)
    )
    summed = jnp.einsum("rhek,rhec->rhkc", placing, received, preferred_element_type=jnp.float32)
    weight_sum = jnp.sum(placing.astype(jnp.float32), axis=2)
    return (summed, weight_sum)


def partial_block(query_rows, key_rows, value_rows, allowed):
    scale_factor = 1.0 / math.sqrt(query_rows.shape[-1])
    scores = (
        jnp.einsum("rhqd,rhkd->rhqk", query_rows, key_rows, preferred_element_type=jnp.float32)
        * scale_factor
    )
    scores = jnp.where(allowed, scores, -1e30)
    highest = jnp.max(scores, axis=-1)
    exponent = jnp.exp(scores - highest[..., None])
    exponent_sum = jnp.sum(exponent, axis=-1)
    weighted = jnp.einsum(
        "rhqk,rhkd->rhqd",
        exponent.astype(jnp.bfloat16),
        value_rows,
        preferred_element_type=jnp.float32,
    )
    return (highest, exponent_sum, weighted)


def body(cache, evicted, merge_weight, targets, kept_counts, queries, new_rows):
    req_local, head_local, kept_dev, width = cache.shape
    head_dim = width // 2
    shard_count = lax.axis_size("seq")
    evict_dev = evicted.shape[2]
    capacity = max(2, 2 * evict_dev // shard_count)
    holder = targets // kept_dev
    position = targets - holder * kept_dev
    owners = (holder[..., None] == jnp.arange(shard_count, dtype=jnp.int32)).astype(jnp.int32)
    earlier = jnp.cumsum(owners, axis=2) - owners
    ranking = jnp.sum(owners * earlier, axis=-1)
    slot_index = holder * capacity + ranking
    packing = slot_index[..., None] == jnp.arange(shard_count * capacity, dtype=jnp.int32)
    packing_matrix = packing.astype(jnp.bfloat16)
    sent_rows = jnp.einsum(
        "rhes,rhec->rhsc", packing_matrix, evicted, preferred_element_type=jnp.float32
    )
    sent_rows = sent_rows.astype(jnp.bfloat16).reshape(
        req_local, head_local, shard_count, capacity, width
    )
    sent_weight = jnp.einsum(
        "rhes,rhe->rhs", packing_matrix, merge_weight, preferred_element_type=jnp.float32
    )
    sent_weight = sent_weight.astype(jnp.bfloat16).reshape(
        req_local, head_local, shard_count, capacity
    )
    sent_position = jnp.sum(jnp.where(packing, position[..., None], 0), axis=2)
    sent_position = sent_position.reshape(req_local, head_local, shard_count, capacity)
    got_rows, got_weight, got_position = (
        lax.all_to_all(sent_rows, "seq", split_axis=2, concat_axis=2, tiled=True),
        lax.all_to_all(sent_weight, "seq", split_axis=2, concat_axis=2, tiled=True),
        lax.all_to_all(sent_position, "seq", split_axis=2, concat_axis=2, tiled=True),
    )
    slot_total = shard_count * capacity
    summed, weight_sum = spread_rows(
        got_rows.reshape(req_local, head_local, slot_total, width),
        got_weight.reshape(req_local, head_local, slot_total),
        got_position.reshape(req_local, head_local, slot_total),
        kept_dev,
    )
    merged = ((cache.astype(jnp.float32) + summed) / (1.0 + weight_sum)[..., None]).astype(
        jnp.bfloat16
    )
    step_count, _, query_local, _ = queries.shape
    group_size = query_local // head_local
    query_rows = queries.reshape(step_count, req_local, head_local, group_size, head_dim).transpose(
        1, 2, 0, 3, 4
    )
    query_rows = query_rows.reshape(req_local, head_local, step_count * group_size, head_dim)
    living = jnp.arange(kept_dev, dtype=jnp.int32)[None, :] < kept_counts
    cache_max, cache_sum, cache_acc = partial_block(
        query_rows, merged[..., :head_dim], merged[..., head_dim:], living[:, None, None, :]
    )
    shared = combined_all((cache_max, cache_sum, cache_acc), "seq", combine_parts)
    fresh_rows = new_rows.transpose(1, 2, 0, 3)
    step_index = jnp.arange(step_count * group_size, dtype=jnp.int32) // group_size
    allowed = jnp.arange(step_count, dtype=jnp.int32)[None, :] <= step_index[:, None]
    fresh_part = partial_block(
        query_rows, fresh_rows[..., :head_dim], fresh_rows[..., head_dim:], allowed[None, None]
    )
    highest, weight_total, weighted = combine_parts(shared, fresh_part)
    result = (weighted / weight_total[..., None]).astype(jnp.bfloat16)
    attended = result.reshape(req_local, head_local, step_count, group_size, head_dim).transpose(
        2, 0, 1, 3, 4
    )
    attended = attended.reshape(step_count, req_local, query_local, head_dim)
    return (merged, attended)


def solution(mesh):
    return jax.shard_map(
        body,
        mesh=mesh,
        in_specs=(
            P(("grp", "req"), "hd", "seq", None),
            P(("grp", "req"), "hd", "seq", None),
            P(("grp", "req"), "hd", "seq"),
            P(("grp", "req"), "hd", "seq"),
            P(("grp", "req"), "seq"),
            P(None, ("grp", "req"), "hd", None),
            P(None, ("grp", "req"), "hd", None),
        ),
        out_specs=(P(("grp", "req"), "hd", "seq", None), P(None, ("grp", "req"), "hd", None)),
        check_vma=False,
    )
```

profile of v0, /device:TPU:0, one launch (start us, length us, event | category | flops | bytes accessed | tf_op | source)
XLA Modules:
  0.0 84.7 jit_solution(8849968173791281850)
XLA Ops:
  0.6 0.7 multiply_subtract_fusion
  1.5 0.3 reduce_window_sum.11
  1.8 0.3 select_reduce_fusion.1
  2.1 0.9 %fusion.20 = f32[2,4,1,128]{3,2,1,0:T(1,128)S(1)} fusion(s32[2,4,64]{2,1,0:T(4,128)S(1)} %multiply_add_fusion.1, bf16[2,4,64,1]{2,1,0,3:T(4,128)(2,1)} %bitcast.96), kind=kOutput, calls=%fused_computation.34 | convolution fusion | flops 196608 | bytes 7168 | tf_op jit(solution)/shard_map/rhes,rhe->rhs/dot_general | solution.py:82
  3.2 0.7 reshape.114
  3.8 6.3 %all-to-all-start.1 = ((bf16[4,2,128]{2,1,0:T(2,128)(2,1)}), bf16[4,2,128]{2,1,0:T(2,128)(2,1)S(1)}, u32[]{:S(2)}, u32[]{:S(2)}) async-start(bf16[4,2,128]{2,1,0:T(2,128)(2,1)} %reshape.114), calls=%async_computation.1 | async-start | bytes 4096 | tf_op jit(solution)/shard_map/all_to_all | solution.py:92
  10.2 0.5 convolution_convert_fusion
  10.7 0.2 select_reduce_fusion
  11.0 0.7 reshape.112
  11.7 4.0 %all-to-all-done.1 = bf16[4,2,128]{2,1,0:T(2,128)(2,1)S(1)} async-done(((bf16[4,2,128]{2,1,0:T(2,128)(2,1)}), bf16[4,2,128]{2,1,0:T(2,128)(2,1)S(1)}, u32[]{:S(2)}, u32[]{:S(2)}) %all-to-all-start.1) | async-done | bytes 2080 | tf_op jit(solution)/shard_map/all_to_all | solution.py:92
  15.7 3.2 %all-to-all-start = ((s32[4,1,256]{2,1,0:T(1,128)}), s32[4,1,256]{2,1,0:T(1,128)S(1)}, u32[]{:S(2)}, u32[]{:S(2)}) async-start(s32[4,1,256]{2,1,0:T(1,128)} %reshape.112), calls=%async_computation | async-start | bytes 8192 | tf_op jit(solution)/shard_map/all_to_all | solution.py:93
  19.0 0.8 copy.21
  19.8 4.7 %all-to-all-done = s32[4,1,256]{2,1,0:T(1,128)S(1)} async-done(((s32[4,1,256]{2,1,0:T(1,128)}), s32[4,1,256]{2,1,0:T(1,128)S(1)}, u32[]{:S(2)}, u32[]{:S(2)}) %all-to-all-start) | async-done | bytes 4128 | tf_op jit(solution)/shard_map/all_to_all | solution.py:93
  24.5 3.5 %all-to-all-start.2 = ((bf16[2,4,4,32,256]{4,3,1,0,2:T(8,128)(2,1)}), bf16[2,4,4,32,256]{4,3,1,0,2:T(8,128)(2,1)S(1)}, u32[]{:S(2)}, u32[]{:S(2)}) async-start(bf16[2,4,4,32,256]{4,3,1,0,2:T(8,128)(2,1)} %copy.21), calls=%async_computation.2 | async-start | bytes 1048576 | tf_op jit(solution)/shard_map/all_to_all | solution.py:91
  28.0 0.2 fusion.45
  28.4 0.5 broadcast.82
  28.9 0.7 reduce
  29.8 0.5 convert_reduce_fusion
  30.3 9.8 %all-to-all-done.2 = bf16[2,4,4,32,256]{4,3,1,0,2:T(8,128)(2,1)S(1)} async-done(((bf16[2,4,4,32,256]{4,3,1,0,2:T(8,128)(2,1)}), bf16[2,4,4,32,256]{4,3,1,0,2:T(8,128)(2,1)S(1)}, u32[]{:S(2)}, u32[]{:S(2)}) %all-to-all-start.2) | async-done | bytes 524320 | tf_op jit(solution)/shard_map/all_to_all | solution.py:91
  40.2 0.8 divide_convert_fusion
  41.0 0.5 fusion.44
  41.5 13.2 %all-gather = f32[8,4,32]{2,1,0:T(4,128)S(1)} all-gather(f32[2,4,32]{2,1,0:T(4,128)S(1)} %get-tuple-element.206), channel_id=2, replica_groups=mesh['grp'=2,'seq'=4,'req'=2,'hd'=2] {'seq'}, dimensions={0}, use_global_device_ids=true | all-gather | bytes 5120 | tf_op jit(solution)/shard_map/all_gather | solution.py:10
  54.7 0.2 fusion.19
  54.9 0.3 fusion.12
  55.2 13.2 %all-gather.1 = f32[8,4,32]{2,1,0:T(4,128)S(1)} all-gather(f32[2,4,32]{2,1,0:T(4,128)S(1)} %fusion.19), channel_id=3, replica_groups=mesh['grp'=2,'seq'=4,'req'=2,'hd'=2] {'seq'}, dimensions={0}, use_global_device_ids=true | all-gather | bytes 5120 | tf_op jit(solution)/shard_map/all_gather | solution.py:10
  68.5 14.7 %all-gather.2 = f32[8,4,32,128]{3,2,1,0:T(8,128)S(1)} all-gather(f32[2,4,32,128]{3,2,1,0:T(8,128)S(1)} %fusion.12), channel_id=4, replica_groups=mesh['grp'=2,'seq'=4,'req'=2,'hd'=2] {'seq'}, dimensions={0}, use_global_device_ids=true | all-gather | bytes 655360 | tf_op jit(solution)/shard_map/all_gather | solution.py:10
  83.1 0.7 while.19
  83.2 0.2 fusion.53
  83.4 0.2 fusion.53
  83.6 0.2 fusion.53
  83.8 0.3 fusion.9
  84.1 0.6 copy.46
  (39 shorter events, 1.0 us)
Async XLA Ops:
  0.6 9.6 %copy-start = (bf16[2,4,64,256]{3,2,1,0:T(8,128)(2,1)S(1)}, bf16[2,4,64,256]{3,2,1,0:T(8,128)(2,1)}, u32[]{:S(2)}) copy-start(bf16[2,4,64,256]{3,2,1,0:T(8,128)(2,1)} %param.10) | copy-start | bytes 786436
  1.4 18.4 %copy-start.2 = (bf16[4,2,4,256]{3,2,1,0:T(4,128)(2,1)S(1)}, bf16[4,2,4,256]{3,2,1,0:T(4,128)(2,1)}, u32[]{:S(2)}) copy-start(bf16[4,2,4,256]{3,2,1,0:T(4,128)(2,1)} %param.15) | copy-start | bytes 49156
  3.1 24.9 %copy-start.5 = (bf16[4,2,32,128]{3,2,1,0:T(8,128)(2,1)S(1)}, bf16[4,2,32,128]{3,2,1,0:T(8,128)(2,1)}, u32[]{:S(2)}) copy-start(bf16[4,2,32,128]{3,2,1,0:T(8,128)(2,1)} %param.14) | copy-start | bytes 196612
  3.8 11.8 %all-to-all-start.1 = ((bf16[4,2,128]{2,1,0:T(2,128)(2,1)}), bf16[4,2,128]{2,1,0:T(2,128)(2,1)S(1)}, u32[]{:S(2)}, u32[]{:S(2)}) async-start(bf16[4,2,128]{2,1,0:T(2,128)(2,1)} %reshape.114), calls=%async_computation.1 | async-start | bytes 4096 | tf_op jit(solution)/shard_map/all_to_all | solution.py:92
  10.2 18.0 %copy-start.3 = (s32[2,1]{0,1:T(1,128)S(1)}, s32[2,1]{0,1:T(1,128)}, u32[]{:S(2)}) copy-start(s32[2,1]{0,1:T(1,128)} %param.13) | copy-start | bytes 28
  15.7 8.8 %all-to-all-start = ((s32[4,1,256]{2,1,0:T(1,128)}), s32[4,1,256]{2,1,0:T(1,128)S(1)}, u32[]{:S(2)}, u32[]{:S(2)}) async-start(s32[4,1,256]{2,1,0:T(1,128)} %reshape.112), calls=%async_computation | async-start | bytes 8192 | tf_op jit(solution)/shard_map/all_to_all | solution.py:93
  18.9 21.2 %copy-start.4 = (bf16[2,4,384,256]{3,2,1,0:T(8,128)(2,1)S(1)}, bf16[2,4,384,256]{3,2,1,0:T(8,128)(2,1)}, u32[]{:S(2)}) copy-start(bf16[2,4,384,256]{3,2,1,0:T(8,128)(2,1)} %param.9) | copy-start | bytes 4718596
  24.5 15.6 %all-to-all-start.2 = ((bf16[2,4,4,32,256]{4,3,1,0,2:T(8,128)(2,1)}), bf16[2,4,4,32,256]{4,3,1,0,2:T(8,128)(2,1)S(1)}, u32[]{:S(2)}, u32[]{:S(2)}) async-start(bf16[2,4,4,32,256]{4,3,1,0,2:T(8,128)(2,1)} %copy.21), calls=%async_computation.2 | async-start | bytes 1048576 | tf_op jit(solution)/shard_map/all_to_all | solution.py:91
  41.0 14.2 %copy-start.1 = (bf16[2,4,384,256]{3,2,1,0:T(8,128)(2,1)}, bf16[2,4,384,256]{3,2,1,0:T(8,128)(2,1)S(1)}, u32[]{:S(2)}) copy-start(bf16[2,4,384,256]{3,2,1,0:T(8,128)(2,1)S(1)} %divide_convert_fusion) | copy-start | bytes 4718596
where the time goes:
time: 85.1 us; the launch traced here: 84.7 us
  blocking collectives  41.1 us (48%)
  waiting for transfers between devices  18.4 us (22%)
  starting transfers between devices  13.1 us (15%)
  local copies, waits for them, and re-layouts  3.97 us (5%)
  other arithmetic  3.78 us (4%)
  matrix products  3.47 us (4%)
    all_gather x3, blocking collectives, combined_all(): gathered = jax.tree.map(lambda a: lax.all_gather(a, axis), part)  41.1 us
    all_to_all x1, waiting for transfers between devices, body(): lax.all_to_all(sent_rows, 'seq', split_axis=2, concat_axis=2, tiled=True)  9.8 us
    all_to_all x1, starting transfers between devices, body(): lax.all_to_all(sent_weight, 'seq', split_axis=2, concat_axis=2, tiled=True)  6.35 us
    all_to_all x1, waiting for transfers between devices, body(): lax.all_to_all(sent_position, 'seq', split_axis=2, concat_axis=2, tiled=T...  4.68 us
    all_to_all x1, waiting for transfers between devices, body(): lax.all_to_all(sent_weight, 'seq', split_axis=2, concat_axis=2, tiled=True)  3.97 us
    all_to_all x1, starting transfers between devices, body(): lax.all_to_all(sent_rows, 'seq', split_axis=2, concat_axis=2, tiled=True)  3.47 us
    all_to_all x1, starting transfers between devices, body(): lax.all_to_all(sent_position, 'seq', split_axis=2, concat_axis=2, tiled=T...  3.25 us
  transfers between devices with their start and end apart: 3, of which 3 were waited for; matrix products, arithmetic and copies ran while one was open for 6% of the time, Pallas kernels for 0%

commit v1 on v0

v1 whole, which is shorter than its diff:
```python
import functools
import math

import jax
import jax.numpy as jnp
from jax import lax
from jax.experimental import pallas as pl
from jax.experimental.pallas import tpu as pltpu
from jax.sharding import PartitionSpec as P

F32 = jnp.float32
BF16 = jnp.bfloat16
NEG = -1e30


def contract_last(a, b):
    return lax.dot_general(a, b, (((1,), (1,)), ((), ())), preferred_element_type=F32)


def softmax_block(query, keys, values, allowed, scale):
    scores = jnp.where(allowed, contract_last(query, keys) * scale, NEG)
    highest = jnp.max(scores, axis=-1, keepdims=True)
    exponent = jnp.exp(scores - highest)
    total = jnp.sum(exponent, axis=-1, keepdims=True)
    weighted = jnp.dot(exponent.astype(BF16), values, preferred_element_type=F32)
    return highest, total, weighted


def kernel(
    shards, cap, groups, owners,
    cache, evicted, weight, target, counts, queries, fresh,
    merged, attended,
    cache_v, evict_v, weight_v, target_v, counts_v, query_v, fresh_v,
    send, recv, meta_send, meta_recv, query_s, fresh_o, fresh_ml,
    part, part_recv, result, attended_v,
    in_sem, cache_sem, out_sem, att_sem, row_ssem, row_rsem, meta_ssem, meta_rsem,
    part_ssem, part_rsem, res_ssem, res_rsem,
):
    reqs, heads, kept, width = cache_v.shape
    pairs = reqs * heads
    evict = evict_v.shape[2]
    steps, _, _, depth = query_v.shape
    rows = query_s.shape[1]
    group = rows // steps
    slots = shards * cap
    per = pairs // owners
    scale = 1.0 / math.sqrt(depth)
    me = lax.axis_index("seq")

    def peer(d):
        return lax.rem(me + d, shards)

    def source(d):
        return lax.rem(me + shards - d, shards)

    def remote(src, dst, ssem, rsem, device):
        return pltpu.make_async_remote_copy(
            src_ref=src, dst_ref=dst, send_sem=ssem, recv_sem=rsem,
            device_id={"seq": device}, device_id_type=pl.DeviceIdType.MESH,
        )

    small = [
        pltpu.make_async_copy(src, dst, in_sem.at[i])
        for i, (src, dst) in enumerate((
            (target, target_v), (weight, weight_v), (evicted, evict_v),
            (queries, query_v), (fresh, fresh_v), (counts, counts_v),
        ))
    ]
    for copy in small:
        copy.start()
    order = []
    for o in [0] + list(range(owners - 1, 0, -1)):
        order += [o * per + j for j in range(per)]
    loads = {}
    for i in order:
        r, h = divmod(i, heads)
        loads[i] = pltpu.make_async_copy(cache.at[r, h], cache_v.at[r, h], cache_sem.at[i])
        loads[i].start()

    barrier = pltpu.get_barrier_semaphore()
    for d in range(1, shards):
        pl.semaphore_signal(
            barrier, inc=1, device_id={"seq": peer(d)}, device_id_type=pl.DeviceIdType.MESH
        )

    for copy in small[:3]:
        copy.wait()
    aimed = jnp.concatenate([target_v[r] for r in range(reqs)], axis=0)
    weights = jnp.concatenate([weight_v[r].astype(F32) for r in range(reqs)], axis=0)
    owned, position, base = [], jnp.zeros_like(aimed), jnp.zeros(aimed.shape, F32)
    for d in range(shards):
        low = peer(d) * kept
        mine = (aimed >= low) & (aimed < low + kept)
        owned.append(jnp.where(mine, 1.0, 0.0))
        position = jnp.where(mine, aimed - low, position)
        base = jnp.where(mine, float(d * cap), base)
    above = lax.broadcasted_iota(jnp.int32, (evict, evict), 0) < lax.broadcasted_iota(
        jnp.int32, (evict, evict), 1
    )
    earlier = jnp.dot(
        jnp.concatenate(owned, axis=0).astype(BF16),
        jnp.where(above, 1.0, 0.0).astype(BF16),
        preferred_element_type=F32,
    )
    slot = base
    for d in range(shards):
        slot = slot + owned[d] * earlier[d * pairs : (d + 1) * pairs]
    slot = slot.astype(jnp.int32)
    features = jnp.concatenate(
        [weights, (position & 255).astype(F32), (position >> 8).astype(F32)], axis=0
    ).astype(BF16)
    slot_row = lax.broadcasted_iota(jnp.int32, (slots, evict), 0)
    for i in order:
        r, h = divmod(i, heads)
        packing = jnp.where(slot_row == slot[i : i + 1, :], 1.0, 0.0).astype(BF16)
        packed = jnp.dot(packing, evict_v[r, h], preferred_element_type=F32).astype(BF16)
        send[i] = packed
        recv[i, 0:cap, :] = packed[0:cap]
        meta = contract_last(features, packing)
        meta_send[i : i + 1, :] = meta[i : i + 1]
        meta_send[pairs + i : pairs + i + 1, :] = (
            meta[2 * pairs + i : 2 * pairs + i + 1] * 256.0 + meta[pairs + i : pairs + i + 1]
        )

    pl.semaphore_wait(barrier, shards - 1)

    meta_copies = {}
    for d in range(1, shards):
        meta_copies[d] = remote(
            meta_send, meta_recv.at[d], meta_ssem.at[d], meta_rsem.at[d], peer(d)
        )
        meta_copies[d].start()
    span = pairs // groups
    row_copies = {}
    for g in range(groups):
        first = order[g] if groups == pairs else g * span
        for d in range(1, shards):
            lot = (pl.ds(first, span), pl.ds(d * cap, cap))
            row_copies[first, d] = remote(
                send.at[lot], recv.at[lot], row_ssem.at[g, d], row_rsem.at[g, d], peer(d)
            )
            row_copies[first, d].start()

    for copy in small[3:]:
        copy.wait()
    diagonal = lax.broadcasted_iota(jnp.int32, (rows, 128), 0) == lax.broadcasted_iota(
        jnp.int32, (rows, 128), 1
    )

    def to_rows(*columns):
        flat = [jnp.sum(jnp.where(diagonal, c, 0.0), axis=0, keepdims=True) for c in columns]
        return jnp.concatenate(flat + [jnp.zeros((8 - len(flat), 128), F32)], axis=0)

    def to_column(row):
        return jnp.sum(jnp.where(diagonal, row, 0.0), axis=1, keepdims=True)

    padded = -(-steps // 16) * 16
    new_step = lax.broadcasted_iota(jnp.int32, (rows, padded), 1)
    row_index = lax.broadcasted_iota(jnp.int32, (rows, padded), 0)
    allowed = row_index < 0
    for s in range(steps):
        allowed = allowed | ((new_step == s) & (row_index >= s * group))
    for r in range(reqs):
        asked = [query_v[s, r].astype(F32) for s in range(steps)]
        added = [fresh_v[s, r].astype(F32) for s in range(steps)]
        for h in range(heads):
            i = r * heads + h
            query = jnp.concatenate(
                [a[h * group : (h + 1) * group] for a in asked], axis=0
            ).astype(BF16)
            query_s[i] = query
            latest = jnp.concatenate(
                [a[h : h + 1] for a in added] + [jnp.zeros((padded - steps, width), F32)], axis=0
            ).astype(BF16)
            highest, total, weighted = softmax_block(
                query, latest[:, :depth], latest[:, depth:], allowed, scale
            )
            fresh_o[i] = weighted
            fresh_ml[i] = to_rows(highest, total)

    for d in range(1, shards):
        meta_copies[d].wait_recv()
    lane = lax.broadcasted_iota(jnp.int32, (2 * pairs, slots), 1)
    meta = meta_send[...]
    for d in range(1, shards):
        meta = jnp.where(lane >= d * cap, meta_recv[d], meta)
    slot_weight = meta[:pairs]
    slot_position = meta[pairs:].astype(jnp.int32)

    kept_row = lax.broadcasted_iota(jnp.int32, (kept, slots), 0)
    kept_lane = lax.broadcasted_iota(jnp.int32, (rows, kept), 1)
    ones = jnp.ones((slots, 128), BF16)
    stores = []
    for n, i in enumerate(order):
        r, h = divmod(i, heads)
        loads[i].wait()
        if groups == pairs:
            for d in range(1, shards):
                row_copies[i, d].wait_recv()
        elif n == 0:
            for copy in row_copies.values():
                copy.wait_recv()
        placing = jnp.where(
            kept_row == slot_position[i : i + 1], slot_weight[i : i + 1], 0.0
        ).astype(BF16)
        summed = jnp.dot(placing, recv[i], preferred_element_type=F32)
        factor = 1.0 / (1.0 + jnp.dot(placing, ones, preferred_element_type=F32))
        factor = jnp.concatenate([factor] * (width // 128), axis=1)
        fused = ((cache_v[r, h].astype(F32) + summed) * factor).astype(BF16)
        cache_v[r, h] = fused
        store = pltpu.make_async_copy(cache_v.at[r, h], merged.at[r, h], out_sem.at[i])
        store.start()
        stores.append(store)
        highest, total, weighted = softmax_block(
            query_s[i], fused[:, :depth], fused[:, depth:], kept_lane < counts_v[r : r + 1, :], scale
        )
        part[i, 0:rows, :] = weighted
        part[i, rows : rows + 8, :] = to_rows(highest, total)
        owner, j = divmod(i, per)
        away = lax.rem(owner - me + shards, shards)

        @pl.when(me != owner)
        def _():
            remote(
                part.at[i], part_recv.at[j, away], part_ssem.at[i], part_rsem.at[j, away], owner
            ).start()

    def part_in(j, d):
        return remote(
            part.at[j], part_recv.at[j, d], part_ssem.at[j], part_rsem.at[j, d], peer(d)
        )

    def res_out(j, d):
        mine = me * per + j
        return remote(
            result.at[mine], result.at[mine], res_ssem.at[j, d], res_rsem.at[j, d], peer(d)
        )

    def res_in(j, d):
        theirs = source(d) * per + j
        return remote(
            result.at[theirs], result.at[theirs], res_ssem.at[j, d], res_rsem.at[j, d], peer(d)
        )

    def only_owners(index, f):
        if owners == shards:
            f()
        else:
            pl.when(index < owners)(f)

    def combine():
        for j in range(per):
            mine = me * per + j
            for d in range(1, shards):
                part_in(j, d).wait_recv()
            tiles = [fresh_ml[mine], part[mine, rows : rows + 8, :]]
            outs = [fresh_o[mine], part[mine, 0:rows, :]]
            for d in range(1, shards):
                tiles.append(part_recv[j, d, rows : rows + 8, :])
                outs.append(part_recv[j, d, 0:rows, :])
            top = tiles[0][0:1]
            for tile in tiles[1:]:
                top = jnp.maximum(top, tile[0:1])
            shares = [jnp.exp(tile[0:1] - top) for tile in tiles]
            total = shares[0] * tiles[0][1:2]
            for share, tile in zip(shares[1:], tiles[1:]):
                total = total + share * tile[1:2]
            lanes = lax.broadcasted_iota(jnp.int32, total.shape, 1)
            total = jnp.where(lanes < rows, total, 1.0)
            blend = to_column(shares[0] / total) * outs[0]
            for share, out in zip(shares[1:], outs[1:]):
                blend = blend + to_column(share / total) * out
            result[mine] = blend.astype(BF16)
            for d in range(1, shards):
                res_out(j, d).start()

    only_owners(me, combine)

    for j in range(per):
        for d in range(1, shards):
            only_owners(source(d), lambda: res_in(j, d).wait_recv())
    for r in range(reqs):
        done = [result[r * heads + h].astype(F32) for h in range(heads)]
        for s in range(steps):
            attended_v[s, r] = jnp.concatenate(
                [a[s * group : (s + 1) * group] for a in done], axis=0
            ).astype(BF16)
    last = pltpu.make_async_copy(attended_v, attended, att_sem.at[0])
    last.start()

    for copy in list(meta_copies.values()) + list(row_copies.values()):
        copy.wait_send()
    for i in order:
        owner = i // per

        @pl.when(me != owner)
        def _():
            remote(
                part.at[i], part_recv.at[0, 1], part_ssem.at[i], part_rsem.at[0, 1], owner
            ).wait_send()

    def drain():
        for j in range(per):
            for d in range(1, shards):
                res_out(j, d).wait_send()

    only_owners(me, drain)
    for store in stores:
        store.wait()
    last.wait()


def body(shards, cache, evicted, merge_weight, targets, kept_counts, queries, new_rows):
    reqs, heads, kept, width = cache.shape
    pairs = reqs * heads
    evict = evicted.shape[2]
    steps, _, query_local, depth = queries.shape
    rows = steps * query_local // heads
    cap = -(-max(2, 2 * evict // shards) // 16) * 16
    slots = shards * cap
    groups = pairs if shards <= 8 else 1
    owners = min(shards, pairs)
    per = pairs // owners
    dma = pltpu.SemaphoreType.DMA
    return pl.pallas_call(
        functools.partial(kernel, shards, cap, groups, owners),
        out_shape=(
            jax.ShapeDtypeStruct(cache.shape, BF16),
            jax.ShapeDtypeStruct(queries.shape, BF16),
        ),
        in_specs=[pl.BlockSpec(memory_space=pl.ANY)] * 7,
        out_specs=(pl.BlockSpec(memory_space=pl.ANY),) * 2,
        scratch_shapes=[
            pltpu.VMEM(cache.shape, BF16),
            pltpu.VMEM(evicted.shape, BF16),
            pltpu.VMEM(merge_weight.shape, BF16),
            pltpu.VMEM(targets.shape, jnp.int32),
            pltpu.VMEM(kept_counts.shape, jnp.int32),
            pltpu.VMEM(queries.shape, BF16),
            pltpu.VMEM(new_rows.shape, BF16),
            pltpu.VMEM((pairs, slots, width), BF16),
            pltpu.VMEM((pairs, slots, width), BF16),
            pltpu.VMEM((2 * pairs, slots), F32),
            pltpu.VMEM((shards, 2 * pairs, slots), F32),
            pltpu.VMEM((pairs, rows, depth), BF16),
            pltpu.VMEM((pairs, rows, depth), F32),
            pltpu.VMEM((pairs, 8, 128), F32),
            pltpu.VMEM((pairs, rows + 8, depth), F32),
            pltpu.VMEM((per, shards, rows + 8, depth), F32),
            pltpu.VMEM((pairs, rows, depth), BF16),
            pltpu.VMEM(queries.shape, BF16),
            dma((6,)),
            dma((pairs,)),
            dma((pairs,)),
            dma((1,)),
            dma((groups, shards)),
            dma((groups, shards)),
            dma((shards,)),
            dma((shards,)),
            dma((pairs,)),
            dma((per, shards)),
            dma((per, shards)),
            dma((per, shards)),
        ],
        compiler_params=pltpu.CompilerParams(
            collective_id=0, has_side_effects=True, vmem_limit_bytes=48 * 1024 * 1024
        ),
    )(cache, evicted, merge_weight, targets, kept_counts, queries, new_rows)


def solution(mesh):
    return jax.shard_map(
        functools.partial(body, mesh.shape["seq"]),
        mesh=mesh,
        in_specs=(
            P(("grp", "req"), "hd", "seq", None),
            P(("grp", "req"), "hd", "seq", None),
            P(("grp", "req"), "hd", "seq"),
            P(("grp", "req"), "hd", "seq"),
            P(("grp", "req"), "seq"),
            P(None, ("grp", "req"), "hd", None),
            P(None, ("grp", "req"), "hd", None),
        ),
        out_specs=(P(("grp", "req"), "hd", "seq", None), P(None, ("grp", "req"), "hd", None)),
        check_vma=False,
    )
```

time: 85.1 us -> 39.9 us (0.47)
  blocking collectives: 41.1 us -> 0 us
  Pallas kernels: 0 us -> 31.1 us
  waiting for transfers between devices: 18.4 us -> 0 us
  starting transfers between devices: 13.1 us -> 0 us
  local copies, waits for them, and re-layouts: 3.97 us -> 7.8 us
  other arithmetic: 3.78 us -> 0 us
  matrix products: 3.47 us -> 0 us
    all_gather x3 -> x0, blocking collectives: 41.1 us -> none  [combined_all(): gathered = jax.tree.map(lambda a: lax.all_gather(a, axis), part)]
    pallas_call x0 -> x1, Pallas kernels: none -> 31.1 us  [body(): pl.pallas_call(functools.partial(kernel, shards, cap, groups, owners), ou...]
    all_to_all x3 -> x0, waiting for transfers between devices: 18.4 us -> none  [the longest x1 9.8 us: body(): lax.all_to_all(sent_rows, 'seq', split_axis=2, concat_axis=2, tiled=True)]
    all_to_all x3 -> x0, starting transfers between devices: 13.1 us -> none  [the longest x1 6.35 us: body(): lax.all_to_all(sent_weight, 'seq', split_axis=2, concat_axis=2, tiled=True)]
    unnamed x17 -> x15, local copies, waits for them, and re-layouts: 1.57 us -> 7.8 us
    dot_general x7 -> x0, matrix products: 3.47 us -> none  [the longest x1 0.93 us: body(): jnp.einsum('rhes,rhe->rhs', packing_matrix, merge_weight, preferred_eleme...]
    reduce_sum x5 -> x0, other arithmetic: 1.3 us -> none  [the longest x1 0.51 us: spread_rows(): weight_sum = jnp.sum(placing.astype(jnp.float32), axis=2)]
    reshape x5 -> x0, local copies, waits for them, and re-layouts: 1.01 us -> none  [the longest x1 0.83 us: body(): sent_rows.astype(jnp.bfloat16)]
  transfers between devices with their start and end apart: 3 -> 0, of which waited for: 3 -> 0; matrix products, arithmetic and copies ran while one was open for 6% -> 0% of each run, Pallas kernels for 0% -> 0%
where the time goes in v1:
time: 39.9 us; the launch traced here: 39.6 us
  Pallas kernels  31.1 us (78%)
  local copies, waits for them, and re-layouts  7.8 us (20%)
  between operations  0.64 us (2%)
    pallas_call x1, Pallas kernels, body(): pl.pallas_call(functools.partial(kernel, shards, cap, groups, owners), ou...  31.1 us
    unnamed x15, local copies, waits for them, and re-layouts  7.8 us

profile of v1, /device:TPU:0, one launch (start us, length us, event | category | flops | bytes accessed | tf_op | source)
XLA Modules:
  0.0 39.6 jit_solution(865563676815790389)
XLA Ops:
  0.6 0.7 %copy.9.counts = s32[2,1]{1,0:T(2,128)S(1)} copy(s32[2,1]{0,1:T(1,128)} %param.11) | data formatting | bytes 16 | tf_op args[4]
  1.4 0.0 copy-start
  1.4 1.4 %copy-done = bf16[2,4,384,256]{3,2,1,0:T(8,128)(2,1)S(1)} copy-done((bf16[2,4,384,256]{3,2,1,0:T(8,128)(2,1)S(1)}, bf16[2,4,384,256]{3,2,1,0:T(8,128)(2,1)}, u32[]{:S(2)}) %copy-start) | copy-done | bytes 1572888
  2.8 0.0 copy-start.1
  2.8 0.9 %copy-done.1 = bf16[2,4,64,256]{3,2,1,0:T(8,128)(2,1)S(1)} copy-done((bf16[2,4,64,256]{3,2,1,0:T(8,128)(2,1)S(1)}, bf16[2,4,64,256]{3,2,1,0:T(8,128)(2,1)}, u32[]{:S(2)}) %copy-start.1) | copy-done | bytes 262168
  3.7 0.0 copy-start.2
  3.7 0.8 %copy-done.2 = bf16[4,2,32,128]{3,2,1,0:T(8,128)(2,1)S(1)} copy-done((bf16[4,2,32,128]{3,2,1,0:T(8,128)(2,1)S(1)}, bf16[4,2,32,128]{3,2,1,0:T(8,128)(2,1)}, u32[]{:S(2)}) %copy-start.2) | copy-done | bytes 65560
  4.6 0.0 copy-start.3
  4.6 0.7 %copy-done.3 = bf16[4,2,4,256]{3,2,1,0:T(4,128)(2,1)S(1)} copy-done((bf16[4,2,4,256]{3,2,1,0:T(4,128)(2,1)S(1)}, bf16[4,2,4,256]{3,2,1,0:T(4,128)(2,1)}, u32[]{:S(2)}) %copy-start.3) | copy-done | bytes 16408
  5.3 0.0 copy-start.4
  5.3 0.7 %copy-done.4 = s32[2,4,64]{2,1,0:T(4,128)S(1)} copy-done((s32[2,4,64]{2,1,0:T(4,128)S(1)}, s32[2,4,64]{2,1,0:T(4,128)}, u32[]{:S(2)}) %copy-start.4) | copy-done | bytes 2072
  6.0 0.0 copy-start.5
  6.0 0.7 %copy-done.5 = bf16[2,4,64]{2,1,0:T(4,128)(2,1)S(1)} copy-done((bf16[2,4,64]{2,1,0:T(4,128)(2,1)S(1)}, bf16[2,4,64]{2,1,0:T(4,128)(2,1)}, u32[]{:S(2)}) %copy-start.5) | copy-done | bytes 1048
  6.7 31.1 %shard_map.86 = (bf16[2,4,384,256]{3,2,1,0:T(8,128)(2,1)S(1)}, bf16[4,2,32,128]{3,2,1,0:T(8,128)(2,1)S(1)}) custom-call(bf16[2,4,384,256]{3,2,1,0:T(8,128)(2,1)S(1)} %copy-done, bf16[2,4,64,256]{3,2,1,0:T(8,128)(2,1)S(1)} %copy-done.1, bf16[2,4,64]{2,1,0:T(4,128)(2,1)S(1)} %copy-done.5, s32[2,4,64]{2,1,0:T(4,128)S(1)} %copy-done.4, s32[2,1]{1,0:T(2,128)S(1)} %copy.9.counts, ...), custom_call_target="tpu_custom_call" | custom-call | tf_op jit(solution)/shard_map/pallas_call | solution.py:325
  37.8 1.1 %copy.12 = bf16[2,4,384,256]{3,2,1,0:T(8,128)(2,1)} copy(bf16[2,4,384,256]{3,2,1,0:T(8,128)(2,1)S(1)} %get-tuple-element.4) | data formatting | bytes 3145728
  39.0 0.6 %copy.13 = bf16[4,2,32,128]{3,2,1,0:T(8,128)(2,1)} copy(bf16[4,2,32,128]{3,2,1,0:T(8,128)(2,1)S(1)} %get-tuple-element.5) | data formatting | bytes 131072
Async XLA Ops:
  1.4 1.4 %copy-start = (bf16[2,4,384,256]{3,2,1,0:T(8,128)(2,1)S(1)}, bf16[2,4,384,256]{3,2,1,0:T(8,128)(2,1)}, u32[]{:S(2)}) copy-start(bf16[2,4,384,256]{3,2,1,0:T(8,128)(2,1)} %cache.1) | copy-start | bytes 4718596
  2.8 0.9 %copy-start.1 = (bf16[2,4,64,256]{3,2,1,0:T(8,128)(2,1)S(1)}, bf16[2,4,64,256]{3,2,1,0:T(8,128)(2,1)}, u32[]{:S(2)}) copy-start(bf16[2,4,64,256]{3,2,1,0:T(8,128)(2,1)} %evicted.1) | copy-start | bytes 786436
  3.7 0.8 %copy-start.2 = (bf16[4,2,32,128]{3,2,1,0:T(8,128)(2,1)S(1)}, bf16[4,2,32,128]{3,2,1,0:T(8,128)(2,1)}, u32[]{:S(2)}) copy-start(bf16[4,2,32,128]{3,2,1,0:T(8,128)(2,1)} %queries.1) | copy-start | bytes 196612
  4.6 0.7 %copy-start.3 = (bf16[4,2,4,256]{3,2,1,0:T(4,128)(2,1)S(1)}, bf16[4,2,4,256]{3,2,1,0:T(4,128)(2,1)}, u32[]{:S(2)}) copy-start(bf16[4,2,4,256]{3,2,1,0:T(4,128)(2,1)} %fresh.1) | copy-start | bytes 49156
  5.3 0.7 %copy-start.4 = (s32[2,4,64]{2,1,0:T(4,128)S(1)}, s32[2,4,64]{2,1,0:T(4,128)}, u32[]{:S(2)}) copy-start(s32[2,4,64]{2,1,0:T(4,128)} %target.1) | copy-start | bytes 6148
  6.0 0.7 %copy-start.5 = (bf16[2,4,64]{2,1,0:T(4,128)(2,1)S(1)}, bf16[2,4,64]{2,1,0:T(4,128)(2,1)}, u32[]{:S(2)}) copy-start(bf16[2,4,64]{2,1,0:T(4,128)(2,1)} %weight.1) | copy-start | bytes 3076

commit v2 on v1

--- a/solution.py
+++ b/solution.py
@@ -30,13 +30,13 @@
     shards, cap, groups, owners,
     cache, evicted, weight, target, counts, queries, fresh,
     merged, attended,
-    cache_v, evict_v, weight_v, target_v, counts_v, query_v, fresh_v,
+    evict_v, weight_v, target_v, counts_v, query_v, fresh_v,
     send, recv, meta_send, meta_recv, query_s, fresh_o, fresh_ml,
-    part, part_recv, result, attended_v,
-    in_sem, cache_sem, out_sem, att_sem, row_ssem, row_rsem, meta_ssem, meta_rsem,
+    part, part_recv, result,
+    in_sem, cache_sem, row_ssem, row_rsem, meta_ssem, meta_rsem,
     part_ssem, part_rsem, res_ssem, res_rsem,
 ):
-    reqs, heads, kept, width = cache_v.shape
+    reqs, heads, kept, width = merged.shape
     pairs = reqs * heads
     evict = evict_v.shape[2]
     steps, _, _, depth = query_v.shape
@@ -74,7 +74,7 @@
     loads = {}
     for i in order:
         r, h = divmod(i, heads)
-        loads[i] = pltpu.make_async_copy(cache.at[r, h], cache_v.at[r, h], cache_sem.at[i])
+        loads[i] = pltpu.make_async_copy(cache.at[r, h], merged.at[r, h], cache_sem.at[i])
         loads[i].start()
 
     barrier = pltpu.get_barrier_semaphore()
@@ -190,7 +190,6 @@
     kept_row = lax.broadcasted_iota(jnp.int32, (kept, slots), 0)
     kept_lane = lax.broadcasted_iota(jnp.int32, (rows, kept), 1)
     ones = jnp.ones((slots, 128), BF16)
-    stores = []
     for n, i in enumerate(order):
         r, h = divmod(i, heads)
         loads[i].wait()
@@ -206,13 +205,10 @@
         summed = jnp.dot(placing, recv[i], preferred_element_type=F32)
         factor = 1.0 / (1.0 + jnp.dot(placing, ones, preferred_element_type=F32))
         factor = jnp.concatenate([factor] * (width // 128), axis=1)
-        fused = ((cache_v[r, h].astype(F32) + summed) * factor).astype(BF16)
-        cache_v[r, h] = fused
-        store = pltpu.make_async_copy(cache_v.at[r, h], merged.at[r, h], out_sem.at[i])
-        store.start()
-        stores.append(store)
+        fused = ((merged[r, h].astype(F32) + summed) * factor).astype(BF16)
+        merged[r, h] = fused
         highest, total, weighted = softmax_block(
-            query_s[i], fused[:, :depth], fused[:, depth:], kept_lane < counts_v[r : r + 1, :], scale
+            query_s[i], fused[:, :depth], fused[:, depth:], kept_lane < counts_v[:, r : r + 1], scale
         )
         part[i, 0:rows, :] = weighted
         part[i, rows : rows + 8, :] = to_rows(highest, total)
@@ -282,11 +278,9 @@
     for r in range(reqs):
         done = [result[r * heads + h].astype(F32) for h in range(heads)]
         for s in range(steps):
-            attended_v[s, r] = jnp.concatenate(
+            attended[s, r] = jnp.concatenate(
                 [a[s * group : (s + 1) * group] for a in done], axis=0
             ).astype(BF16)
-    last = pltpu.make_async_copy(attended_v, attended, att_sem.at[0])
-    last.start()
 
     for copy in list(meta_copies.values()) + list(row_copies.values()):
         copy.wait_send()
@@ -305,9 +299,17 @@
                 res_out(j, d).wait_send()
 
     only_owners(me, drain)
-    for store in stores:
-        store.wait()
-    last.wait()
+
+
+def write_out(merged, attended, merged_out, attended_out, sem):
+    copies = [
+        pltpu.make_async_copy(merged, merged_out, sem.at[0]),
+        pltpu.make_async_copy(attended, attended_out, sem.at[1]),
+    ]
+    for copy in copies:
+        copy.start()
+    for copy in copies:
+        copy.wait()
 
 
 def body(shards, cache, evicted, merge_weight, targets, kept_counts, queries, new_rows):
@@ -322,20 +324,19 @@
     owners = min(shards, pairs)
     per = pairs // owners
     dma = pltpu.SemaphoreType.DMA
-    return pl.pallas_call(
+    done = pl.pallas_call(
         functools.partial(kernel, shards, cap, groups, owners),
         out_shape=(
             jax.ShapeDtypeStruct(cache.shape, BF16),
             jax.ShapeDtypeStruct(queries.shape, BF16),
         ),
-        in_specs=[pl.BlockSpec(memory_space=pl.ANY)] * 7,
-        out_specs=(pl.BlockSpec(memory_space=pl.ANY),) * 2,
+        in_specs=[pl.BlockSpec(memory_space=pltpu.HBM)] * 7,
+        out_specs=(pl.BlockSpec(memory_space=pltpu.VMEM),) * 2,
         scratch_shapes=[
-            pltpu.VMEM(cache.shape, BF16),
             pltpu.VMEM(evicted.shape, BF16),
             pltpu.VMEM(merge_weight.shape, BF16),
             pltpu.VMEM(targets.shape, jnp.int32),
-            pltpu.VMEM(kept_counts.shape, jnp.int32),
+            pltpu.VMEM(kept_counts.shape[::-1], jnp.int32),
             pltpu.VMEM(queries.shape, BF16),
             pltpu.VMEM(new_rows.shape, BF16),
             pltpu.VMEM((pairs, slots, width), BF16),
@@ -348,11 +349,8 @@
             pltpu.VMEM((pairs, rows + 8, depth), F32),
             pltpu.VMEM((per, shards, rows + 8, depth), F32),
             pltpu.VMEM((pairs, rows, depth), BF16),
-            pltpu.VMEM(queries.shape, BF16),
             dma((6,)),
             dma((pairs,)),
-            dma((pairs,)),
-            dma((1,)),
             dma((groups, shards)),
             dma((groups, shards)),
             dma((shards,)),
@@ -365,7 +363,17 @@
         compiler_params=pltpu.CompilerParams(
             collective_id=0, has_side_effects=True, vmem_limit_bytes=48 * 1024 * 1024
         ),
-    )(cache, evicted, merge_weight, targets, kept_counts, queries, new_rows)
+    )(*(
+        pltpu.with_memory_space_constraint(a, pltpu.HBM)
+        for a in (cache, evicted, merge_weight, targets, kept_counts.T, queries, new_rows)
+    ))
+    return pl.pallas_call(
+        write_out,
+        out_shape=tuple(jax.ShapeDtypeStruct(a.shape, a.dtype) for a in done),
+        in_specs=[pl.BlockSpec(memory_space=pltpu.VMEM)] * 2,
+        out_specs=(pl.BlockSpec(memory_space=pltpu.HBM),) * 2,
+        scratch_shapes=[dma((2,))],
+    )(*(pltpu.with_memory_space_constraint(a, pltpu.VMEM) for a in done))
 
 
 def solution(mesh):

time: 39.9 us -> 30.3 us (0.76)
  local copies, waits for them, and re-layouts: 7.8 us -> 0 us
  Pallas kernels: 31.1 us -> 29.6 us
    unnamed x15 -> x0, local copies, waits for them, and re-layouts: 7.8 us -> none
    pallas_call x1, Pallas kernels: 31.1 us -> 28.4 us  [body(): pl.pallas_call(functools.partial(kernel, shards, cap, groups, owners), ou...]
    pallas_call x0 -> x1, Pallas kernels: none -> 1.17 us  [body(): pl.pallas_call(write_out, out_shape=tuple((jax.ShapeDtypeStruct(a.shape,...]
where the time goes in v2:
time: 30.3 us; the launch traced here: 30.2 us
  Pallas kernels  29.6 us (98%)
  between operations  0.64 us (2%)
    pallas_call x1, Pallas kernels, body(): pl.pallas_call(functools.partial(kernel, shards, cap, groups, owners), ou...  28.4 us
    pallas_call x1, Pallas kernels, body(): pl.pallas_call(write_out, out_shape=tuple((jax.ShapeDtypeStruct(a.shape,...  1.17 us

profile of v2, /device:TPU:0, one launch (start us, length us, event | category | flops | bytes accessed | tf_op | source)
XLA Modules:
  0.0 30.2 jit_solution(2803213368073651645)
XLA Ops:
  0.6 28.4 %shard_map.86 = (bf16[2,4,384,256]{3,2,1,0:T(8,128)(2,1)S(1)}, bf16[4,2,32,128]{3,2,1,0:T(8,128)(2,1)S(1)}) custom-call(bf16[2,4,384,256]{3,2,1,0:T(8,128)(2,1)} %cache.1, bf16[2,4,64,256]{3,2,1,0:T(8,128)(2,1)} %evicted.1, bf16[2,4,64]{2,1,0:T(4,128)(2,1)} %weight.1, s32[2,4,64]{2,1,0:T(4,128)} %target.1, s32[1,2]{1,0:T(1,128)} %bitcast.1, ...), custom_call_target="tpu_custom_call" | custom-call | tf_op jit(solution)/shard_map/pallas_call | solution.py:327
  29.0 1.2 %shard_map.87 = (bf16[2,4,384,256]{3,2,1,0:T(8,128)(2,1)}, bf16[4,2,32,128]{3,2,1,0:T(8,128)(2,1)}) custom-call(bf16[2,4,384,256]{3,2,1,0:T(8,128)(2,1)S(1)} %get-tuple-element.4.merged, bf16[4,2,32,128]{3,2,1,0:T(8,128)(2,1)S(1)} %get-tuple-element.5.attended), custom_call_target="tpu_custom_call" | custom-call | tf_op jit(solution)/shard_map/pallas_call | solution.py:370

commit v3 on v2

--- a/solution.py
+++ b/solution.py
@@ -32,9 +32,9 @@
     merged, attended,
     evict_v, weight_v, target_v, counts_v, query_v, fresh_v,
     send, recv, meta_send, meta_recv, query_s, fresh_o, fresh_ml,
-    part, part_recv, result,
+    part, part_recv, part_all, result,
     in_sem, cache_sem, row_ssem, row_rsem, meta_ssem, meta_rsem,
-    part_ssem, part_rsem, res_ssem, res_rsem,
+    part_ssem, part_rsem, all_ssem, all_rsem, res_ssem, res_rsem,
 ):
     reqs, heads, kept, width = merged.shape
     pairs = reqs * heads
@@ -69,7 +69,8 @@
     for copy in small:
         copy.start()
     order = []
-    for o in [0] + list(range(owners - 1, 0, -1)):
+    shared = min(1, owners - 1)
+    for o in [0] * shared + list(range(owners - 1, shared, -1)) + [shared]:
         order += [o * per + j for j in range(per)]
     loads = {}
     for i in order:
@@ -187,6 +188,12 @@
     slot_weight = meta[:pairs]
     slot_position = meta[pairs:].astype(jnp.int32)
 
+    def part_out(i, d):
+        j = i % per
+        return remote(
+            part.at[i], part_all.at[j, d], all_ssem.at[j, d], all_rsem.at[j, d], peer(d)
+        )
+
     kept_row = lax.broadcasted_iota(jnp.int32, (kept, slots), 0)
     kept_lane = lax.broadcasted_iota(jnp.int32, (rows, kept), 1)
     ones = jnp.ones((slots, 128), BF16)
@@ -213,6 +220,10 @@
         part[i, 0:rows, :] = weighted
         part[i, rows : rows + 8, :] = to_rows(highest, total)
         owner, j = divmod(i, per)
+        if owner == shared:
+            for d in range(1, shards):
+                part_out(i, d).start()
+            continue
         away = lax.rem(owner - me + shards, shards)
 
         @pl.when(me != owner)
@@ -239,38 +250,43 @@
         )
 
     def only_owners(index, f):
-        if owners == shards:
-            f()
-        else:
-            pl.when(index < owners)(f)
+        pl.when((index < owners) & (index != shared))(f)
+
+    def blend_pair(mine, arrived):
+        tiles = [fresh_ml[mine], part[mine, rows : rows + 8, :]]
+        outs = [fresh_o[mine], part[mine, 0:rows, :]]
+        for ref in arrived:
+            tiles.append(ref[rows : rows + 8, :])
+            outs.append(ref[0:rows, :])
+        top = tiles[0][0:1]
+        for tile in tiles[1:]:
+            top = jnp.maximum(top, tile[0:1])
+        shares = [jnp.exp(tile[0:1] - top) for tile in tiles]
+        total = shares[0] * tiles[0][1:2]
+        for share, tile in zip(shares[1:], tiles[1:]):
+            total = total + share * tile[1:2]
+        lanes = lax.broadcasted_iota(jnp.int32, total.shape, 1)
+        total = jnp.where(lanes < rows, total, 1.0)
+        blend = to_column(shares[0] / total) * outs[0]
+        for share, out in zip(shares[1:], outs[1:]):
+            blend = blend + to_column(share / total) * out
+        result[mine] = blend.astype(BF16)
 
     def combine():
         for j in range(per):
             mine = me * per + j
             for d in range(1, shards):
                 part_in(j, d).wait_recv()
-            tiles = [fresh_ml[mine], part[mine, rows : rows + 8, :]]
-            outs = [fresh_o[mine], part[mine, 0:rows, :]]
-            for d in range(1, shards):
-                tiles.append(part_recv[j, d, rows : rows + 8, :])
-                outs.append(part_recv[j, d, 0:rows, :])
-            top = tiles[0][0:1]
-            for tile in tiles[1:]:
-                top = jnp.maximum(top, tile[0:1])
-            shares = [jnp.exp(tile[0:1] - top) for tile in tiles]
-            total = shares[0] * tiles[0][1:2]
-            for share, tile in zip(shares[1:], tiles[1:]):
-                total = total + share * tile[1:2]
-            lanes = lax.broadcasted_iota(jnp.int32, total.shape, 1)
-            total = jnp.where(lanes < rows, total, 1.0)
-            blend = to_column(shares[0] / total) * outs[0]
-            for share, out in zip(shares[1:], outs[1:]):
-                blend = blend + to_column(share / total) * out
-            result[mine] = blend.astype(BF16)
+            blend_pair(mine, [part_recv.at[j, d] for d in range(1, shards)])
             for d in range(1, shards):
                 res_out(j, d).start()
 
     only_owners(me, combine)
+    for j in range(per):
+        i = shared * per + j
+        for d in range(1, shards):
+            part_out(i, d).wait_recv()
+        blend_pair(i, [part_all.at[j, d] for d in range(1, shards)])
 
     for j in range(per):
         for d in range(1, shards):
@@ -286,6 +302,10 @@
         copy.wait_send()
     for i in order:
         owner = i // per
+        if owner == shared:
+            for d in range(1, shards):
+                part_out(i, d).wait_send()
+            continue
 
         @pl.when(me != owner)
         def _():
@@ -348,6 +368,7 @@
             pltpu.VMEM((pairs, 8, 128), F32),
             pltpu.VMEM((pairs, rows + 8, depth), F32),
             pltpu.VMEM((per, shards, rows + 8, depth), F32),
+            pltpu.VMEM((per, shards, rows + 8, depth), F32),
             pltpu.VMEM((pairs, rows, depth), BF16),
             dma((6,)),
             dma((pairs,)),
@@ -356,6 +377,8 @@
             dma((shards,)),
             dma((shards,)),
             dma((pairs,)),
+            dma((per, shards)),
+            dma((per, shards)),
             dma((per, shards)),
             dma((per, shards)),
             dma((per, shards)),

time: 30.3 us -> 31.2 us (1.030)
  Pallas kernels: 29.6 us -> 30.4 us
    pallas_call x1, Pallas kernels: 28.4 us -> 29.2 us  [body(): pl.pallas_call(functools.partial(kernel, shards, cap, groups, owners), ou...]
where the time goes in v3:
time: 31.2 us; the launch traced here: 31 us
  Pallas kernels  30.4 us (97%)
  between operations  0.64 us (2%)
    pallas_call x1, Pallas kernels, body(): pl.pallas_call(functools.partial(kernel, shards, cap, groups, owners), ou...  29.2 us
    pallas_call x1, Pallas kernels, body(): pl.pallas_call(write_out, out_shape=tuple((jax.ShapeDtypeStruct(a.shape,...  1.17 us

profile of v3, /device:TPU:0, one launch (start us, length us, event | category | flops | bytes accessed | tf_op | source)
XLA Modules:
  0.0 31.0 jit_solution(3060374072140257920)
XLA Ops:
  0.6 29.2 %shard_map.86 = (bf16[2,4,384,256]{3,2,1,0:T(8,128)(2,1)S(1)}, bf16[4,2,32,128]{3,2,1,0:T(8,128)(2,1)S(1)}) custom-call(bf16[2,4,384,256]{3,2,1,0:T(8,128)(2,1)} %cache.1, bf16[2,4,64,256]{3,2,1,0:T(8,128)(2,1)} %evicted.1, bf16[2,4,64]{2,1,0:T(4,128)(2,1)} %weight.1, s32[2,4,64]{2,1,0:T(4,128)} %target.1, s32[1,2]{1,0:T(1,128)} %bitcast.1, ...), custom_call_target="tpu_custom_call" | custom-call | tf_op jit(solution)/shard_map/pallas_call | solution.py:347
  29.8 1.2 %shard_map.87 = (bf16[2,4,384,256]{3,2,1,0:T(8,128)(2,1)}, bf16[4,2,32,128]{3,2,1,0:T(8,128)(2,1)}) custom-call(bf16[2,4,384,256]{3,2,1,0:T(8,128)(2,1)S(1)} %get-tuple-element.4.merged, bf16[4,2,32,128]{3,2,1,0:T(8,128)(2,1)S(1)} %get-tuple-element.5.attended), custom_call_target="tpu_custom_call" | custom-call | tf_op jit(solution)/shard_map/pallas_call | solution.py:393

commit v4 on v2

--- a/solution.py
+++ b/solution.py
@@ -32,8 +32,9 @@
     merged, attended,
     evict_v, weight_v, target_v, counts_v, query_v, fresh_v,
     send, recv, meta_send, meta_recv, query_s, fresh_o, fresh_ml,
-    part, part_recv, result,
-    in_sem, cache_sem, row_ssem, row_rsem, meta_ssem, meta_rsem,
+    relay, part, part_recv, result,
+    in_sem, cache_sem, row_ssem, row_rsem, hop_ssem, hop_rsem, fwd_ssem,
+    meta_ssem, meta_rsem,
     part_ssem, part_rsem, res_ssem, res_rsem,
 ):
     reqs, heads, kept, width = merged.shape
@@ -131,15 +132,43 @@
         )
         meta_copies[d].start()
     span = pairs // groups
-    row_copies = {}
-    for g in range(groups):
-        first = order[g] if groups == pairs else g * span
-        for d in range(1, shards):
-            lot = (pl.ds(first, span), pl.ds(d * cap, cap))
-            row_copies[first, d] = remote(
-                send.at[lot], recv.at[lot], row_ssem.at[g, d], row_rsem.at[g, d], peer(d)
-            )
-            row_copies[first, d].start()
+    middle = shards // 2
+    bounce = groups == pairs and shards >= 4 and shards % 2 == 0
+    late = order[pairs - pairs // 2 :] if bounce else []
+
+    def hop_in(k, i):
+        return remote(
+            send.at[i, pl.ds(middle * cap, cap)], relay.at[k],
+            hop_ssem.at[k], hop_rsem.at[k], peer(shards - 1),
+        )
+
+    def hop_out(k, i):
+        return remote(
+            relay.at[k], recv.at[i, pl.ds(middle * cap, cap)],
+            fwd_ssem.at[k], row_rsem.at[order.index(i), middle], peer(middle + 1),
+        )
+
+    for k, i in enumerate(late):
+        hop_in(k, i).start()
+    row_copies, sent = {}, []
+
+    def send_rows(part_of, distances):
+        for g in part_of:
+            first = order[g] if groups == pairs else g * span
+            for d in distances:
+                lot = (pl.ds(first, span), pl.ds(d * cap, cap))
+                copy = remote(
+                    send.at[lot], recv.at[lot], row_ssem.at[g, d], row_rsem.at[g, d], peer(d)
+                )
+                row_copies[first, d] = copy
+                if first in late and d == middle:
+                    continue
+                copy.start()
+                sent.append(copy)
+
+    early = groups - len(late)
+    send_rows(range(early), range(1, shards))
+    send_rows(range(early, groups), range(1, middle + 1))
 
     for copy in small[3:]:
         copy.wait()
@@ -178,6 +207,10 @@
             fresh_o[i] = weighted
             fresh_ml[i] = to_rows(highest, total)
 
+    for k, i in enumerate(late):
+        hop_in(k, i).wait_recv()
+        hop_out(k, i).start()
+    send_rows(range(early, groups), range(middle + 1, shards))
     for d in range(1, shards):
         meta_copies[d].wait_recv()
     lane = lax.broadcasted_iota(jnp.int32, (2 * pairs, slots), 1)
@@ -282,8 +315,11 @@
                 [a[s * group : (s + 1) * group] for a in done], axis=0
             ).astype(BF16)
 
-    for copy in list(meta_copies.values()) + list(row_copies.values()):
+    for copy in list(meta_copies.values()) + sent:
         copy.wait_send()
+    for k, i in enumerate(late):
+        hop_in(k, i).wait_send()
+        hop_out(k, i).wait_send()
     for i in order:
         owner = i // per
 
@@ -346,6 +382,7 @@
             pltpu.VMEM((pairs, rows, depth), BF16),
             pltpu.VMEM((pairs, rows, depth), F32),
             pltpu.VMEM((pairs, 8, 128), F32),
+            pltpu.VMEM((max(1, pairs // 2), cap, width), BF16),
             pltpu.VMEM((pairs, rows + 8, depth), F32),
             pltpu.VMEM((per, shards, rows + 8, depth), F32),
             pltpu.VMEM((pairs, rows, depth), BF16),
@@ -353,6 +390,9 @@
             dma((pairs,)),
             dma((groups, shards)),
             dma((groups, shards)),
+            dma((max(1, pairs // 2),)),
+            dma((max(1, pairs // 2),)),
+            dma((max(1, pairs // 2),)),
             dma((shards,)),
             dma((shards,)),
             dma((pairs,)),

time: 30.3 us -> 31.2 us (1.030)
  Pallas kernels: 29.6 us -> 30.4 us
    pallas_call x1, Pallas kernels: 28.4 us -> 29.2 us  [body(): pl.pallas_call(functools.partial(kernel, shards, cap, groups, owners), ou...]
where the time goes in v4:
time: 31.2 us; the launch traced here: 31 us
  Pallas kernels  30.4 us (97%)
  between operations  0.64 us (2%)
    pallas_call x1, Pallas kernels, body(): pl.pallas_call(functools.partial(kernel, shards, cap, groups, owners), ou...  29.2 us
    pallas_call x1, Pallas kernels, body(): pl.pallas_call(write_out, out_shape=tuple((jax.ShapeDtypeStruct(a.shape,...  1.17 us

profile of v4, /device:TPU:0, one launch (start us, length us, event | category | flops | bytes accessed | tf_op | source)
XLA Modules:
  0.0 31.0 jit_solution(12604633365431310371)
XLA Ops:
  0.6 29.2 %shard_map.86 = (bf16[2,4,384,256]{3,2,1,0:T(8,128)(2,1)S(1)}, bf16[4,2,32,128]{3,2,1,0:T(8,128)(2,1)S(1)}) custom-call(bf16[2,4,384,256]{3,2,1,0:T(8,128)(2,1)} %cache.1, bf16[2,4,64,256]{3,2,1,0:T(8,128)(2,1)} %evicted.1, bf16[2,4,64]{2,1,0:T(4,128)(2,1)} %weight.1, s32[2,4,64]{2,1,0:T(4,128)} %target.1, s32[1,2]{1,0:T(1,128)} %bitcast.1, ...), custom_call_target="tpu_custom_call" | custom-call | tf_op jit(solution)/shard_map/pallas_call | solution.py:363
  29.8 1.2 %shard_map.87 = (bf16[2,4,384,256]{3,2,1,0:T(8,128)(2,1)}, bf16[4,2,32,128]{3,2,1,0:T(8,128)(2,1)}) custom-call(bf16[2,4,384,256]{3,2,1,0:T(8,128)(2,1)S(1)} %get-tuple-element.4.merged, bf16[4,2,32,128]{3,2,1,0:T(8,128)(2,1)S(1)} %get-tuple-element.5.attended), custom_call_target="tpu_custom_call" | custom-call | tf_op jit(solution)/shard_map/pallas_call | solution.py:410
